TPU v7x, 32 devices: a whole 2x2x4 slice. The times are simulated.
32 devices in a mesh: dp: 8 (over z, x), mp: 4 (over y, core).
Axes of the slice: x: 2, y: 2, z: 4, core: 2. Of those that a mesh axis runs over, the one named last changes fastest.
Arguments:
- rows: float32 [16384, 1280], P(('dp', 'mp')), may hold values from -6 to 6
- lengths: int32 [256], P('dp'), may hold values from 1 to 64, as said below
- freq_class: int32 [256], P(('dp', 'mp')), may hold values from 0 to 2
- freq_table: float32 [3, 1280], replicated, may hold values from -3 to 3
- gain_attn: float32 [1280], replicated, may hold values from 0.5 to 1.5
- gain_mlp: float32 [1280], replicated, may hold values from 0.5 to 1.5
- w_qkv: float32 [3, 1280, 1280], P(None, None, 'mp'), may hold values from -0.15625 to 0.15625
- w_out: float32 [1280, 1280], P('mp'), may hold values from -0.5 to 0.5
- w_gate_up: float32 [2, 1280, 5120], P(None, None, 'mp'), may hold values from -0.15625 to 0.15625
- w_down: float32 [5120, 1280], P('mp'), may hold values from -0.15625 to 0.15625
- cotangent: float32 [16384, 1280], P(('dp', 'mp')), may hold values from -6 to 6
Outputs:
- output: float32 [16384, 1280], P(('dp', 'mp'))
- grad_rows: float32 [16384, 1280], P(('dp', 'mp'))
- grad_qkv: float32 [3, 1280, 1280], P(None, None, 'mp')
- grad_out: float32 [1280, 1280], P('mp')
- grad_gate_up: float32 [2, 1280, 5120], P(None, None, 'mp')
- grad_down: float32 [5120, 1280], P('mp')
- grad_gain_attn: float32 [1280], replicated
- grad_gain_mlp: float32 [1280], replicated
- grad_table: float32 [3, 1280], replicated
Inputs may be any that keep to these rules, and one draw needn't show every extreme that they name: `lengths`: the valid patches of a series are the last of its 64 slots; some series has all 64, and some only one.
All inputs are finite; a program needn't handle non-finite values.
Results may differ from a plain program's by a relative error of at most 0.02.
Values may be sent and summed in bfloat16 or wider, within the bound.
A program may use at most 256 MiB of HBM per device.

v0:
```python
import jax
import jax.numpy as jnp
from jax import lax
from jax.sharding import PartitionSpec as P

HS = 80
NFREQ = 3
SEQ = 64
EPSILON = 1e-06
NEGATIVE = -1e30
HIGHEST = lax.Precision.HIGHEST


def rotate(values, cosines, sines):
    half_width = values.shape[-1] // 2
    first_half = values[..., :half_width]
    second_half = values[..., half_width:]
    return jnp.concatenate(
        [first_half * cosines - second_half * sines, second_half * cosines + first_half * sines], -1
    )


def series_tables(series_lengths):
    places = jnp.arange(SEQ, dtype=jnp.int32)
    starts = SEQ - series_lengths
    valid_mask = places[None, :] >= starts[:, None]
    positions = (places[None, :] - starts[:, None]).astype(jnp.float32)
    frequency = 10000.0 ** (-2.0 * jnp.arange(HS // 2, dtype=jnp.float32) / HS)
    angles = positions[:, :, None] * frequency[None, None, :]
    return (valid_mask, jnp.cos(angles)[:, :, None, :], jnp.sin(angles)[:, :, None, :])


def allowed_pairs(valid_mask):
    places = jnp.arange(SEQ, dtype=jnp.int32)
    causal = places[:, None] >= places[None, :]
    itself = places[:, None] == places[None, :]
    return causal[None, None] & (valid_mask[:, None, None, :] | itself[None, None])


def norm_forward(values, gain):
    inverse = lax.rsqrt(jnp.mean(values * values, -1, keepdims=True) + EPSILON)
    return ((values * inverse * gain).astype(jnp.bfloat16), inverse)


def norm_backward(values, inverse, gain, grad_normed):
    normal = values * inverse
    grad_gain = jnp.sum(grad_normed * normal, 0)
    scaled = grad_normed * gain
    grad_values = inverse * (scaled - normal * jnp.mean(scaled * normal, -1, keepdims=True))
    return (grad_values, grad_gain)


def attention_scores(queries, keys, allowed):
    raw_scores = jnp.einsum("sihe,sjhe->shij", queries, keys, preferred_element_type=jnp.float32)
    return jnp.where(allowed, raw_scores * HS ** (-0.5), NEGATIVE)


def body(
    rows,
    lengths,
    freq_class,
    freq_table,
    gain_attn,
    gain_mlp,
    w_qkv,
    w_out,
    w_gate_up,
    w_down,
    cotangent,
):
    local_rows = rows.shape[0]
    mp_index = lax.axis_index("mp")
    series_count = lengths.shape[0]
    group_rows = series_count * SEQ
    heads_width = w_out.shape[0]
    head_count = heads_width // HS
    valid_mask, cosines, sines = series_tables(lengths)
    allowed = allowed_pairs(valid_mask)
    flat_valid = valid_mask.reshape(group_rows).astype(jnp.float32)
    mine_valid = lax.dynamic_slice_in_dim(flat_valid, mp_index * local_rows, local_rows)[:, None]
    classes = jnp.repeat(freq_class, SEQ)
    onehot = (classes[:, None] == jnp.arange(NFREQ, dtype=jnp.int32)[None, :]).astype(jnp.float32)
    start_rows = rows + jnp.dot(onehot, freq_table, precision=HIGHEST)
    normed_mine, inverse_attn = norm_forward(start_rows, gain_attn)
    normed = lax.all_gather(normed_mine, "mp", axis=0, tiled=True)
    qkv_low = w_qkv.astype(jnp.bfloat16)
    projected = jnp.einsum("td,cdf->ctf", normed, qkv_low, preferred_element_type=jnp.float32)
    projected = projected.reshape(3, series_count, SEQ, head_count, HS)
    queries = rotate(projected[0], cosines, sines).astype(jnp.bfloat16)
    keys = rotate(projected[1], cosines, sines).astype(jnp.bfloat16)
    values = projected[2].astype(jnp.bfloat16)
    scores = attention_scores(queries, keys, allowed)
    row_max = jnp.max(scores, -1, keepdims=True)
    exponent = jnp.exp(scores - row_max)
    row_total = jnp.sum(exponent, -1, keepdims=True)
    log_total = row_max + jnp.log(row_total)
    attention = (exponent / row_total).astype(jnp.bfloat16)
    mixed = jnp.einsum("shij,sjhe->sihe", attention, values, preferred_element_type=jnp.float32)
    mixed = mixed.reshape(group_rows, heads_width).astype(jnp.bfloat16)
    out_low = w_out.astype(jnp.bfloat16)
    attn_part = jnp.dot(mixed, out_low, preferred_element_type=jnp.float32)
    after_attn = start_rows + lax.psum_scatter(
        attn_part.astype(jnp.bfloat16), "mp", scatter_dimension=0, tiled=True
    ).astype(jnp.float32)
    normed_mlp_mine, inverse_mlp = norm_forward(after_attn, gain_mlp)
    normed_mlp = lax.all_gather(normed_mlp_mine, "mp", axis=0, tiled=True)
    gate_up_low = w_gate_up.astype(jnp.bfloat16)
    gate_up = jnp.einsum("td,cdf->ctf", normed_mlp, gate_up_low, preferred_element_type=jnp.float32)
    gate_pre = gate_up[0]
    up_pre = gate_up[1]
    sigmoid_gate = jax.nn.sigmoid(gate_pre)
    activated = gate_pre * sigmoid_gate
    hidden = (activated * up_pre).astype(jnp.bfloat16)
    down_low = w_down.astype(jnp.bfloat16)
    mlp_part = jnp.dot(hidden, down_low, preferred_element_type=jnp.float32)
    output = after_attn + lax.psum_scatter(
        mlp_part.astype(jnp.bfloat16), "mp", scatter_dimension=0, tiled=True
    ).astype(jnp.float32)
    grad_output = cotangent * mine_valid
    grad_down_in = lax.all_gather(grad_output.astype(jnp.bfloat16), "mp", axis=0, tiled=True)
    grad_down = jnp.einsum("tf,td->fd", hidden, grad_down_in, preferred_element_type=jnp.float32)
    grad_hidden = jnp.einsum(
        "td,fd->tf", grad_down_in, down_low, preferred_element_type=jnp.float32
    )
    grad_gate = grad_hidden * up_pre * (sigmoid_gate * (1.0 + gate_pre * (1.0 - sigmoid_gate)))
    grad_up = grad_hidden * activated
    grad_pre = jnp.stack([grad_gate, grad_up]).astype(jnp.bfloat16)
    grad_gate_up = jnp.einsum(
        "td,ctf->cdf", normed_mlp, grad_pre, preferred_element_type=jnp.float32
    )
    mlp_back_part = jnp.einsum(
        "ctf,cdf->td", grad_pre, gate_up_low, preferred_element_type=jnp.float32
    )
    grad_normed_mlp = lax.psum_scatter(
        mlp_back_part.astype(jnp.bfloat16), "mp", scatter_dimension=0, tiled=True
    ).astype(jnp.float32)
    grad_rows_mlp, grad_gain_mlp = norm_backward(after_attn, inverse_mlp, gain_mlp, grad_normed_mlp)
    grad_after = grad_output + grad_rows_mlp
    grad_attn_in = lax.all_gather(grad_after.astype(jnp.bfloat16), "mp", axis=0, tiled=True)
    grad_out = jnp.einsum("tf,td->fd", mixed, grad_attn_in, preferred_element_type=jnp.float32)
    grad_mixed = jnp.einsum("td,fd->tf", grad_attn_in, out_low, preferred_element_type=jnp.float32)
    grad_mixed = grad_mixed.astype(jnp.bfloat16).reshape(series_count, SEQ, head_count, HS)
    attention_again = jnp.exp(attention_scores(queries, keys, allowed) - log_total)
    grad_attention = jnp.einsum(
        "sihe,sjhe->shij", grad_mixed, values, preferred_element_type=jnp.float32
    )
    grad_values = jnp.einsum(
        "shij,sihe->sjhe",
        attention_again.astype(jnp.bfloat16),
        grad_mixed,
        preferred_element_type=jnp.float32,
    )
    row_dot = jnp.sum(attention_again * grad_attention, -1, keepdims=True)
    grad_scores = (attention_again * (grad_attention - row_dot)).astype(jnp.bfloat16)
    grad_queries = jnp.einsum(
        "shij,sjhe->sihe", grad_scores, keys, preferred_element_type=jnp.float32
    ) * HS ** (-0.5)
    grad_keys = jnp.einsum(
        "shij,sihe->sjhe", grad_scores, queries, preferred_element_type=jnp.float32
    ) * HS ** (-0.5)
    grad_projected = jnp.stack(
        [rotate(grad_queries, cosines, -sines), rotate(grad_keys, cosines, -sines), grad_values]
    )
    grad_projected = grad_projected.reshape(3, group_rows, heads_width).astype(jnp.bfloat16)
    grad_qkv = jnp.einsum("td,ctf->cdf", normed, grad_projected, preferred_element_type=jnp.float32)
    attn_back_part = jnp.einsum(
        "ctf,cdf->td", grad_projected, qkv_low, preferred_element_type=jnp.float32
    )
    grad_normed = lax.psum_scatter(
        attn_back_part.astype(jnp.bfloat16), "mp", scatter_dimension=0, tiled=True
    ).astype(jnp.float32)
    grad_rows_attn, grad_gain_attn = norm_backward(start_rows, inverse_attn, gain_attn, grad_normed)
    grad_rows = grad_after + grad_rows_attn
    grad_table = jnp.dot(onehot.T, grad_rows, precision=HIGHEST)
    grad_gain_attn, grad_gain_mlp, grad_table, token_total = lax.psum(
        (grad_gain_attn, grad_gain_mlp, grad_table, jnp.sum(mine_valid)), ("dp", "mp")
    )
    grad_qkv, grad_out, grad_gate_up, grad_down = (
        lax.psum(grad_qkv.astype(jnp.bfloat16), "dp").astype(jnp.float32),
        lax.psum(grad_out.astype(jnp.bfloat16), "dp").astype(jnp.float32),
        lax.psum(grad_gate_up.astype(jnp.bfloat16), "dp").astype(jnp.float32),
        lax.psum(grad_down.astype(jnp.bfloat16), "dp").astype(jnp.float32),
    )
    root_scale = lax.rsqrt(token_total)
    return (
        output,
        grad_rows,
        grad_qkv * root_scale,
        grad_out * root_scale,
        grad_gate_up * root_scale,
        grad_down * root_scale,
        grad_gain_attn * root_scale,
        grad_gain_mlp * root_scale,
        grad_table * root_scale,
    )


def solution(mesh):
    return jax.shard_map(
        body,
        mesh=mesh,
        in_specs=(
            P(("dp", "mp"), None),
            P("dp"),
            P(("dp", "mp")),
            P(),
            P(),
            P(),
            P(None, None, "mp"),
            P("mp", None),
            P(None, None, "mp"),
            P("mp", None),
            P(("dp", "mp"), None),
        ),
        out_specs=(
            P(("dp", "mp"), None),
            P(("dp", "mp"), None),
            P(None, None, "mp"),
            P("mp", None),
            P(None, None, "mp"),
            P("mp", None),
            P(),
            P(),
            P(),
        ),
        check_vma=False,
    )
```

profile of v0, /device:TPU:0, one launch (start us, length us, event | category | flops | bytes accessed | tf_op | source)
XLA Modules:
  0.0 1067.2 jit_solution(17084121526547978977)
XLA Ops:
  13.6 5.8 fusion.48
  19.4 36.9 %all-gather.5.cloned.1.call-done = bf16[2048,1280]{1,0:T(8,128)(2,1)} async-done(((bf16[512,1280]{1,0:T(8,128)(2,1)}), bf16[2048,1280]{1,0:T(8,128)(2,1)}) %all-gather.5.cloned.1.call-update) | async-done | bytes 5242896 | tf_op jit(solution)/shard_map/all_gather | solution.py:85
  56.3 8.7 fusion.10
  78.8 5.3 reshape.177
  84.1 5.5 fusion.62
  99.3 5.3 reshape.178
  104.7 5.5 fusion.63
  119.9 7.9 subtract_convert_fusion.3
  143.1 7.1 convolution_convert_fusion.2
  150.3 51.5 %reduce-scatter.5.cloned.1.call-done = bf16[512,1280]{1,0:T(8,128)(2,1)} async-done(((bf16[2048,1280]{1,0:T(8,128)(2,1)}), bf16[512,1280]{1,0:T(8,128)(2,1)}) %reduce-scatter.5.cloned.1.call-update) | async-done | bytes 1310736 | tf_op jit(solution)/shard_map/reduce_scatter | solution.py:102
  208.6 38.5 %all-gather.7.cloned.1.call-done = bf16[2048,1280]{1,0:T(8,128)(2,1)} async-done(((bf16[512,1280]{1,0:T(8,128)(2,1)}), bf16[2048,1280]{1,0:T(8,128)(2,1)}) %all-gather.7.cloned.1.call-update) | async-done | bytes 5242896 | tf_op jit(solution)/shard_map/all_gather | solution.py:106
  247.0 22.6 %convolution_bitcast_fusion = f32[2,2048,1280]{2,1,0:T(8,128)} fusion(bf16[2048,1280]{1,0:T(8,128)(2,1)} %all-gather.7.cloned.1.call-done, f32[2,1280,1280]{2,1,0:T(8,128)} %param.19), kind=kOutput, calls=%fused_computation.1 | convolution fusion | flops 13425049600 | bytes 39321600 | tf_op jit(solution)/shard_map/td,cdf->ctf/dot_general | solution.py:108
  269.6 20.0 %all-gather.9.cloned.1.call-done = bf16[2048,1280]{1,0:T(8,128)(2,1)} async-done(((bf16[512,1280]{1,0:T(8,128)(2,1)}), bf16[2048,1280]{1,0:T(8,128)(2,1)}) %all-gather.9.cloned.1.call-update) | async-done | bytes 5242896 | tf_op jit(solution)/shard_map/all_gather | solution.py:120
  289.6 21.7 %fusion.9 = (bf16[1,2048,1280]{2,1,0:T(8,128)(2,1)}, bf16[1,2048,1280]{2,1,0:T(8,128)(2,1)}, bf16[2048,1280]{1,0:T(8,128)(2,1)}) fusion(f32[2,2048,1280]{2,1,0:T(8,128)} %convolution_bitcast_fusion, bf16[2048,1280]{1,0:T(8,128)(2,1)} %all-gather.9.cloned.1.call-done, f32[1280,1280]{1,0:T(8,128)} %param.20), kind=kOutput, calls=%fused_computation.25 | convolution fusion | flops 6751846400 | bytes 48496640 | tf_op jit(solution)/shard_map/td,fd->tf/dot_general | solution.py:122
  311.2 21.7 %bitcast_convert_fusion.1 = bf16[2048,1280]{1,0:T(8,128)(2,1)} fusion(bf16[1,2048,1280]{2,1,0:T(8,128)(2,1)} %get-tuple-element.46, bf16[1,2048,1280]{2,1,0:T(8,128)(2,1)} %get-tuple-element.45, f32[2,1280,1280]{2,1,0:T(8,128)} %param.19), kind=kOutput, calls=%fused_computation.7 | convolution fusion | flops 13432913920 | bytes 28835840 | tf_op jit(solution)/shard_map/ctf,cdf->td/dot_general | solution.py:131
  333.0 12.4 %convolution_convert_fusion.1 = bf16[2048,1280]{1,0:T(8,128)(2,1)} fusion(bf16[2048,1280]{1,0:T(8,128)(2,1)} %get-tuple-element.47, f32[1280,1280]{1,0:T(8,128)} %param.20), kind=kOutput, calls=%fused_computation.14 | convolution fusion | flops 6715146240 | bytes 17039360 | tf_op jit(solution)/shard_map/dot_general | solution.py:115
  345.4 39.1 %reduce-scatter.9.cloned.1.call-done = bf16[512,1280]{1,0:T(8,128)(2,1)} async-done(((bf16[2048,1280]{1,0:T(8,128)(2,1)}), bf16[512,1280]{1,0:T(8,128)(2,1)}) %reduce-scatter.9.cloned.1.call-update) | async-done | bytes 1310736 | tf_op jit(solution)/shard_map/reduce_scatter | solution.py:134
  386.7 51.7 %reduce-scatter.7.cloned.1.call-done = bf16[512,1280]{1,0:T(8,128)(2,1)} async-done(((bf16[2048,1280]{1,0:T(8,128)(2,1)}), bf16[512,1280]{1,0:T(8,128)(2,1)}) %reduce-scatter.7.cloned.1.call-update) | async-done | bytes 1310736 | tf_op jit(solution)/shard_map/reduce_scatter | solution.py:116
  438.4 6.3 fusion.59
  444.8 40.5 %all-gather.11.cloned.1.call-done = bf16[2048,1280]{1,0:T(8,128)(2,1)} async-done(((bf16[512,1280]{1,0:T(8,128)(2,1)}), bf16[2048,1280]{1,0:T(8,128)(2,1)}) %all-gather.11.cloned.1.call-update) | async-done | bytes 5242896 | tf_op jit(solution)/shard_map/all_gather | solution.py:139
  517.1 5.0 copy.59
  525.2 5.0 copy.60
  537.7 5.0 copy.58
  550.5 9.9 bitcast_convert_fusion
  560.5 12.3 %convolution_convert_fusion.3 = bf16[1280,1280]{1,0:T(8,128)(2,1)} fusion(bf16[2048,1280]{1,0:T(8,128)(2,1)} %get-tuple-element.47, bf16[2048,1280]{1,0:T(8,128)(2,1)} %all-gather.9.cloned.1.call-done), kind=kOutput, calls=%fused_computation.16 | convolution fusion | flops 6712524800 | bytes 13762560 | tf_op jit(solution)/shard_map/tf,td->fd/dot_general | solution.py:121
  572.8 20.2 %fusion.1 = bf16[2,1280,1280]{1,2,0:T(8,128)(2,1)} fusion(bf16[1,2048,1280]{2,1,0:T(8,128)(2,1)} %get-tuple-element.46, bf16[1,2048,1280]{2,1,0:T(8,128)(2,1)} %get-tuple-element.45, bf16[2048,1280]{1,0:T(8,128)(2,1)} %all-gather.7.cloned.1.call-done), kind=kOutput, calls=%fused_computation.13 | convolution fusion | flops 13430292480 | bytes 22282240 | tf_op jit(solution)/shard_map/td,ctf->cdf/dot_general | solution.py:128
  595.9 6.5 fusion.20
  602.5 9.5 reduce-scatter.11.cloned.1.call-done
  617.7 44.2 %all-reduce = (f32[]{:T(128)}, f32[1280]{0:T(1024)S(1)}, f32[1280]{0:T(1024)S(1)}, f32[3,1280]{1,0:T(4,128)S(1)}) all-reduce(f32[]{:T(128)} %get-tuple-element.39, f32[1280]{0:T(1024)S(1)} %get-tuple-element.29, f32[1280]{0:T(1024)S(1)} %get-tuple-element.27, f32[3,1280]{1,0:T(4,128)S(1)} %fusion.49), channel_id=1, replica_groups=mesh['dp'=8,'mp'=4] {'dp','mp'}, use_global_device_ids=true, to_apply=%region_13.14 | all-reduce | flops 6401 | bytes 51208 | tf_op jit(solution)/shard_map/psum | solution.py:175
  664.4 365.7 %all-reduce.4.cloned.1.call-done = (bf16[3,1280,320]{1,2,0:T(8,128)(2,1)}, bf16[320,1280]{1,0:T(8,128)(2,1)}, bf16[2,1280,1280]{1,2,0:T(8,128)(2,1)}, bf16[1280,1280]{1,0:T(8,128)(2,1)}) async-done(((bf16[3,1280,320]{1,2,0:T(8,128)(2,1)}, bf16[320,1280]{1,0:T(8,128)(2,1)}, bf16[2,1280,1280]{1,2,0:T(8,128)(2,1)}, bf16[1280,1280]{1,0:T(8,128)(2,1)}), (bf16[3,1280,320]{1,2,0:T(8,128)(2,1)}, ...) | async-done | bytes 13107216 | tf_op jit(solution)/shard_map/psum | solution.py:179
  1040.7 5.8 convert_multiply_fusion
  1046.5 13.9 %copy.54 = f32[2,1280,1280]{2,1,0:T(8,128)} copy(f32[2,1280,1280]{1,2,0:T(8,128)} %convert_multiply_fusion) | data formatting | bytes 26214400
  (170 shorter events, 135.1 us)
Async XLA Ops:
  7.2 4.1 copy-start.31
  7.2 49.1 %all-gather.5.cloned.1.call-start = ((), (), s32[]{:S(2)}) async-start(), calls=%async_computation.4 | async-start | bytes 6553600 | tf_op jit(solution)/shard_map/all_gather | solution.py:85
  8.1 4.9 copy-start.35
  11.3 190.5 %copy-start.4 = (f32[512,1280]{1,0:T(8,128)}, f32[512,1280]{1,0:T(8,128)S(1)}, u32[]{:S(2)}) copy-start(f32[512,1280]{1,0:T(8,128)S(1)} %get-tuple-element.73) | copy-start | bytes 7864324
  13.0 188.8 %reduce-scatter.5.cloned.1.call-start = ((), (), s32[]{:S(2)}) async-start(), calls=%async_computation.5 | async-start | bytes 6553600 | tf_op jit(solution)/shard_map/reduce_scatter | solution.py:102
  127.9 3.3 copy-start.8
  127.9 3.3 copy-start.14
  131.2 4.3 copy-start.2
  150.2 54.8 %copy-start.30 = (f32[1280]{0:T(1024)S(1)}, f32[1280]{0:T(1024)}, u32[]{:S(2)}) copy-start(f32[1280]{0:T(1024)} %param.16) | copy-start | bytes 15364
  150.2 96.8 %all-gather.7.cloned.1.call-start = ((), (), s32[]{:S(2)}) async-start(), calls=%async_computation.6 | async-start | bytes 6553600 | tf_op jit(solution)/shard_map/all_gather | solution.py:106
  203.6 3.7 copy-start.18
  206.4 83.1 %all-gather.9.cloned.1.call-start = ((), (), s32[]{:S(2)}) async-start(), calls=%async_computation.8 | async-start | bytes 6553600 | tf_op jit(solution)/shard_map/all_gather | solution.py:120
  208.5 176.0 %reduce-scatter.9.cloned.1.call-start = ((), (), s32[]{:S(2)}) async-start(), calls=%async_computation.9 | async-start | bytes 6553600 | tf_op jit(solution)/shard_map/reduce_scatter | solution.py:134
  333.0 105.4 %reduce-scatter.7.cloned.1.call-start = ((), (), s32[]{:S(2)}) async-start(), calls=%async_computation.7 | async-start | bytes 6553600 | tf_op jit(solution)/shard_map/reduce_scatter | solution.py:116
  345.4 39.1 %copy-start.7 = (f32[512,1280]{1,0:T(8,128)S(1)}, f32[512,1280]{1,0:T(8,128)}, u32[]{:S(2)}) copy-start(f32[512,1280]{1,0:T(8,128)} %copy-done.6) | copy-start | bytes 7864324
  345.4 139.9 %all-gather.11.cloned.1.call-start = ((), (), s32[]{:S(2)}) async-start(), calls=%async_computation.10 | async-start | bytes 6553600 | tf_op jit(solution)/shard_map/all_gather | solution.py:139
  444.7 167.3 %reduce-scatter.11.cloned.1.call-start = ((), (), s32[]{:S(2)}) async-start(), calls=%async_computation.11 | async-start | bytes 6553600 | tf_op jit(solution)/shard_map/reduce_scatter | solution.py:169
  497.8 4.5 copy-start.3
  497.8 4.5 copy-start.21
  560.4 469.8 %all-reduce.4.cloned.1.call-start = ((), (), s32[]{:S(2)}) async-start(), calls=%async_computation.12 | async-start | bytes 26214400 | tf_op jit(solution)/shard_map/psum | solution.py:179
  560.4 32.6 %slice-start.4 = ((s8[5242880]{0:T(1024)(128)(4,1)}), s8[4194304]{0:T(1024)(128)(4,1)S(1)}, s32[]{:S(2)}) async-start(s8[5242880]{0:T(1024)(128)(4,1)} %bitcast.110), calls=%async_computation.17 | async-start | bytes 8388608
  560.5 35.5 %slice-start.2 = ((s8[5242880]{0:T(1024)(128)(4,1)}), s8[4194304]{0:T(1024)(128)(4,1)S(1)}, s32[]{:S(2)}) async-start(s8[5242880]{0:T(1024)(128)(4,1)} %bitcast.108), calls=%async_computation.15 | async-start | bytes 8388608
  572.8 20.3 %copy-start.27 = (bf16[2048,320]{1,0:T(8,128)(2,1)S(1)}, bf16[2048,320]{1,0:T(8,128)(2,1)}, u32[]{:S(2)}) copy-start(bf16[2048,320]{1,0:T(8,128)(2,1)} %convert_element_type.131) | copy-start | bytes 3932164
  572.8 20.3 %slice-start.5 = ((s8[5242880]{0:T(1024)(128)(4,1)}), s8[1048576]{0:T(1024)(128)(4,1)S(1)}, s32[]{:S(2)}) async-start(s8[5242880]{0:T(1024)(128)(4,1)} %bitcast.110), calls=%async_computation.18 | async-start | bytes 2097152
  572.8 23.1 %slice-start.3 = ((s8[5242880]{0:T(1024)(128)(4,1)}), s8[1048576]{0:T(1024)(128)(4,1)S(1)}, s32[]{:S(2)}) async-start(s8[5242880]{0:T(1024)(128)(4,1)} %bitcast.108), calls=%async_computation.16 | async-start | bytes 2097152
  602.5 9.5 copy-start.5
  602.5 9.5 copy-start.32
  602.5 9.5 copy-start.34
  1032.7 3.3 copy-start.25
  1032.7 7.0 slice-start
  1036.0 4.7 slice-start.1
  1046.5 13.9 %copy-start.1 = (f32[3,1280]{1,0:T(4,128)S(1)}, f32[3,1280]{1,0:T(4,128)}, u32[]{:S(2)}) copy-start(f32[3,1280]{1,0:T(4,128)} %param.14) | copy-start | bytes 46084
  (21 other events, 45.5 us)
Sparse Core Ops, SparseCore 0:
  13.1 43.1 all-gather.4
  150.3 51.3 reduce-scatter.4
  206.5 40.4 all-gather.6
  249.1 40.4 all-gather.8
  333.1 51.3 reduce-scatter.8
  386.9 51.3 reduce-scatter.6
  444.8 40.4 all-gather.10
  560.5 51.3 reduce-scatter.10
  617.3 412.7 all-reduce.3
where the time goes:
time: 1080 us; the launch traced here: 1070 us
  waiting for transfers between devices  653 us (60%)
  matrix products  168 us (16%)
  local copies, waits for them, and re-layouts  122 us (11%)
  other arithmetic  63.7 us (6%)
  blocking collectives  44.2 us (4%)
  between operations  15.3 us (1%)
    psum x1, waiting for transfers between devices, body(): lax.psum(grad_qkv.astype(jnp.bfloat16), 'dp').astype(jnp.float32)  366 us
    reduce_scatter x1, waiting for transfers between devices, body(): lax.psum_scatter(mlp_part.astype(jnp.bfloat16), 'mp', scatter_dimension=0...  51.7 us
    reduce_scatter x1, waiting for transfers between devices, body(): lax.psum_scatter(attn_part.astype(jnp.bfloat16), 'mp', scatter_dimension=...  51.5 us
    unnamed x95, local copies, waits for them, and re-layouts  46.5 us
    psum x1, blocking collectives, body(): lax.psum((grad_gain_attn, grad_gain_mlp, grad_table, jnp.sum(mine_valid))...  44.2 us
    all_gather x1, waiting for transfers between devices, body(): lax.all_gather(grad_after.astype(jnp.bfloat16), 'mp', axis=0, tiled=True)  40.5 us
    reduce_scatter x1, waiting for transfers between devices, body(): lax.psum_scatter(mlp_back_part.astype(jnp.bfloat16), 'mp', scatter_dimens...  39.1 us
    all_gather x1, waiting for transfers between devices, body(): normed_mlp = lax.all_gather(normed_mlp_mine, 'mp', axis=0, tiled=True)  38.5 us
  transfers between devices with their start and end apart: 9, of which 9 were waited for; matrix products, arithmetic and copies ran while one was open for 9% of the time, Pallas kernels for 0%

commit v1 on v0

--- a/solution.py
+++ b/solution.py
@@ -173,7 +173,7 @@
     grad_rows = grad_after + grad_rows_attn
     grad_table = jnp.dot(onehot.T, grad_rows, precision=HIGHEST)
     grad_gain_attn, grad_gain_mlp, grad_table, token_total = lax.psum(
-        (grad_gain_attn, grad_gain_mlp, grad_table, jnp.sum(mine_valid)), ("dp", "mp")
+        lax.psum((grad_gain_attn, grad_gain_mlp, grad_table, jnp.sum(mine_valid)), "mp"), "dp"
     )
     grad_qkv, grad_out, grad_gate_up, grad_down = (
         lax.psum(grad_qkv.astype(jnp.bfloat16), "dp").astype(jnp.float32),

time: 1080 us -> 1080 us (level)
    psum x0 -> x1, blocking collectives: none -> 41.7 us  [body(): lax.psum(lax.psum((grad_gain_attn, grad_gain_mlp, grad_table, jnp.sum(min...]
    psum x1, blocking collectives: 44.2 us -> 11.9 us  [body(): lax.psum((grad_gain_attn, grad_gain_mlp, grad_table, jnp.sum(mine_valid))...]
where the time goes in v1:
time: 1080 us; the launch traced here: 1070 us
  waiting for transfers between devices  644 us (60%)
  matrix products  169 us (16%)
  local copies, waits for them, and re-layouts  122 us (11%)
  other arithmetic  63.7 us (6%)
  blocking collectives  53.6 us (5%)
  between operations  15.3 us (1%)
    psum x1, waiting for transfers between devices, body(): lax.psum(grad_qkv.astype(jnp.bfloat16), 'dp').astype(jnp.float32)  357 us
    reduce_scatter x1, waiting for transfers between devices, body(): lax.psum_scatter(mlp_part.astype(jnp.bfloat16), 'mp', scatter_dimension=0...  51.7 us
    reduce_scatter x1, waiting for transfers between devices, body(): lax.psum_scatter(attn_part.astype(jnp.bfloat16), 'mp', scatter_dimension=...  51.5 us
    unnamed x95, local copies, waits for them, and re-layouts  46.5 us
    psum x1, blocking collectives, body(): lax.psum(lax.psum((grad_gain_attn, grad_gain_mlp, grad_table, jnp.sum(min...  41.7 us
    all_gather x1, waiting for transfers between devices, body(): lax.all_gather(grad_after.astype(jnp.bfloat16), 'mp', axis=0, tiled=True)  40.5 us
    reduce_scatter x1, waiting for transfers between devices, body(): lax.psum_scatter(mlp_back_part.astype(jnp.bfloat16), 'mp', scatter_dimens...  39.1 us
    all_gather x1, waiting for transfers between devices, body(): normed_mlp = lax.all_gather(normed_mlp_mine, 'mp', axis=0, tiled=True)  38.5 us
  transfers between devices with their start and end apart: 9, of which 9 were waited for; matrix products, arithmetic and copies ran while one was open for 9% of the time, Pallas kernels for 0%

profile of v1, /device:TPU:0, one launch (start us, length us, event | category | flops | bytes accessed | tf_op | source)
XLA Modules:
  0.0 1067.4 jit_solution(10487443622468101147)
XLA Ops:
  13.6 5.8 fusion.48
  19.4 36.9 %all-gather.5.cloned.1.call-done = bf16[2048,1280]{1,0:T(8,128)(2,1)} async-done(((bf16[512,1280]{1,0:T(8,128)(2,1)}), bf16[2048,1280]{1,0:T(8,128)(2,1)}) %all-gather.5.cloned.1.call-update) | async-done | bytes 5242896 | tf_op jit(solution)/shard_map/all_gather | solution.py:85
  56.3 8.7 fusion.10
  78.8 5.3 reshape.177
  84.1 5.5 fusion.62
  99.3 5.3 reshape.178
  104.7 5.5 fusion.63
  119.9 7.9 subtract_convert_fusion.3
  143.1 7.1 convolution_convert_fusion.2
  150.3 51.5 %reduce-scatter.5.cloned.1.call-done = bf16[512,1280]{1,0:T(8,128)(2,1)} async-done(((bf16[2048,1280]{1,0:T(8,128)(2,1)}), bf16[512,1280]{1,0:T(8,128)(2,1)}) %reduce-scatter.5.cloned.1.call-update) | async-done | bytes 1310736 | tf_op jit(solution)/shard_map/reduce_scatter | solution.py:102
  208.6 38.5 %all-gather.7.cloned.1.call-done = bf16[2048,1280]{1,0:T(8,128)(2,1)} async-done(((bf16[512,1280]{1,0:T(8,128)(2,1)}), bf16[2048,1280]{1,0:T(8,128)(2,1)}) %all-gather.7.cloned.1.call-update) | async-done | bytes 5242896 | tf_op jit(solution)/shard_map/all_gather | solution.py:106
  247.0 22.7 %convolution_bitcast_fusion = f32[2,2048,1280]{2,1,0:T(8,128)} fusion(bf16[2048,1280]{1,0:T(8,128)(2,1)} %all-gather.7.cloned.1.call-done, f32[2,1280,1280]{2,1,0:T(8,128)} %param.19), kind=kOutput, calls=%fused_computation.1 | convolution fusion | flops 13425049600 | bytes 39321600 | tf_op jit(solution)/shard_map/td,cdf->ctf/dot_general | solution.py:108
  269.7 19.9 %all-gather.9.cloned.1.call-done = bf16[2048,1280]{1,0:T(8,128)(2,1)} async-done(((bf16[512,1280]{1,0:T(8,128)(2,1)}), bf16[2048,1280]{1,0:T(8,128)(2,1)}) %all-gather.9.cloned.1.call-update) | async-done | bytes 5242896 | tf_op jit(solution)/shard_map/all_gather | solution.py:120
  289.6 21.7 %fusion.9 = (bf16[1,2048,1280]{2,1,0:T(8,128)(2,1)}, bf16[1,2048,1280]{2,1,0:T(8,128)(2,1)}, bf16[2048,1280]{1,0:T(8,128)(2,1)}) fusion(f32[2,2048,1280]{2,1,0:T(8,128)} %convolution_bitcast_fusion, bf16[2048,1280]{1,0:T(8,128)(2,1)} %all-gather.9.cloned.1.call-done, f32[1280,1280]{1,0:T(8,128)} %param.20), kind=kOutput, calls=%fused_computation.25 | convolution fusion | flops 6751846400 | bytes 48496640 | tf_op jit(solution)/shard_map/td,fd->tf/dot_general | solution.py:122
  311.2 21.7 %bitcast_convert_fusion.1 = bf16[2048,1280]{1,0:T(8,128)(2,1)} fusion(bf16[1,2048,1280]{2,1,0:T(8,128)(2,1)} %get-tuple-element.50, bf16[1,2048,1280]{2,1,0:T(8,128)(2,1)} %get-tuple-element.49, f32[2,1280,1280]{2,1,0:T(8,128)} %param.19), kind=kOutput, calls=%fused_computation.7 | convolution fusion | flops 13432913920 | bytes 28835840 | tf_op jit(solution)/shard_map/ctf,cdf->td/dot_general | solution.py:131
  333.0 12.3 %convolution_convert_fusion.1 = bf16[2048,1280]{1,0:T(8,128)(2,1)} fusion(bf16[2048,1280]{1,0:T(8,128)(2,1)} %get-tuple-element.51, f32[1280,1280]{1,0:T(8,128)} %param.20), kind=kOutput, calls=%fused_computation.14 | convolution fusion | flops 6715146240 | bytes 17039360 | tf_op jit(solution)/shard_map/dot_general | solution.py:115
  345.4 39.1 %reduce-scatter.9.cloned.1.call-done = bf16[512,1280]{1,0:T(8,128)(2,1)} async-done(((bf16[2048,1280]{1,0:T(8,128)(2,1)}), bf16[512,1280]{1,0:T(8,128)(2,1)}) %reduce-scatter.9.cloned.1.call-update) | async-done | bytes 1310736 | tf_op jit(solution)/shard_map/reduce_scatter | solution.py:134
  386.7 51.7 %reduce-scatter.7.cloned.1.call-done = bf16[512,1280]{1,0:T(8,128)(2,1)} async-done(((bf16[2048,1280]{1,0:T(8,128)(2,1)}), bf16[512,1280]{1,0:T(8,128)(2,1)}) %reduce-scatter.7.cloned.1.call-update) | async-done | bytes 1310736 | tf_op jit(solution)/shard_map/reduce_scatter | solution.py:116
  438.3 6.3 fusion.59
  444.7 40.5 %all-gather.11.cloned.1.call-done = bf16[2048,1280]{1,0:T(8,128)(2,1)} async-done(((bf16[512,1280]{1,0:T(8,128)(2,1)}), bf16[2048,1280]{1,0:T(8,128)(2,1)}) %all-gather.11.cloned.1.call-update) | async-done | bytes 5242896 | tf_op jit(solution)/shard_map/all_gather | solution.py:139
  517.1 5.0 copy.59
  537.7 5.0 copy.58
  550.5 9.9 bitcast_convert_fusion
  560.5 12.3 %convolution_convert_fusion.3 = bf16[1280,1280]{1,0:T(8,128)(2,1)} fusion(bf16[2048,1280]{1,0:T(8,128)(2,1)} %get-tuple-element.51, bf16[2048,1280]{1,0:T(8,128)(2,1)} %all-gather.9.cloned.1.call-done), kind=kOutput, calls=%fused_computation.16 | convolution fusion | flops 6712524800 | bytes 13762560 | tf_op jit(solution)/shard_map/tf,td->fd/dot_general | solution.py:121
  572.8 20.2 %fusion.1 = bf16[2,1280,1280]{1,2,0:T(8,128)(2,1)} fusion(bf16[1,2048,1280]{2,1,0:T(8,128)(2,1)} %get-tuple-element.50, bf16[1,2048,1280]{2,1,0:T(8,128)(2,1)} %get-tuple-element.49, bf16[2048,1280]{1,0:T(8,128)(2,1)} %all-gather.7.cloned.1.call-done), kind=kOutput, calls=%fused_computation.13 | convolution fusion | flops 13430292480 | bytes 22282240 | tf_op jit(solution)/shard_map/td,ctf->cdf/dot_general | solution.py:128
  595.9 6.5 fusion.20
  602.5 9.4 reduce-scatter.11.cloned.1.call-done
  617.7 11.9 %all-reduce.1 = (f32[]{:T(128)}, f32[1280]{0:T(1024)S(1)}, f32[1280]{0:T(1024)S(1)}, f32[3,1280]{1,0:T(4,128)S(1)}) all-reduce(f32[]{:T(128)} %get-tuple-element.43, f32[1280]{0:T(1024)S(1)} %get-tuple-element.29, f32[1280]{0:T(1024)S(1)} %get-tuple-element.27, f32[3,1280]{1,0:T(4,128)S(1)} %fusion.49), channel_id=1, replica_groups=mesh['dp'=8,'mp'=4] {'mp'}, use_global_device_ids=true, to_apply=%region_13.14 | all-reduce | flops 6401 | bytes 51208 | tf_op jit(solution)/shard_map/psum | solution.py:176
  629.6 41.7 %all-reduce = (f32[]{:T(128)}, f32[1280]{0:T(1024)S(1)}, f32[1280]{0:T(1024)S(1)}, f32[3,1280]{1,0:T(4,128)S(1)}) all-reduce(f32[]{:T(128)} %get-tuple-element.35, f32[1280]{0:T(1024)S(1)} %get-tuple-element.36, f32[1280]{0:T(1024)S(1)} %get-tuple-element.37, f32[3,1280]{1,0:T(4,128)S(1)} %get-tuple-element.38), channel_id=1, replica_groups=mesh['dp'=8,'mp'=4] {'dp'}, use_global_device_ids=true, to_apply=%region_14.15 | all-reduce | flops 6401 | bytes 51208 | tf_op jit(solution)/shard_map/psum | solution.py:175
  673.8 356.6 %all-reduce.5.cloned.1.call-done = (bf16[3,1280,320]{1,2,0:T(8,128)(2,1)}, bf16[320,1280]{1,0:T(8,128)(2,1)}, bf16[2,1280,1280]{1,2,0:T(8,128)(2,1)}, bf16[1280,1280]{1,0:T(8,128)(2,1)}) async-done(((bf16[3,1280,320]{1,2,0:T(8,128)(2,1)}, bf16[320,1280]{1,0:T(8,128)(2,1)}, bf16[2,1280,1280]{1,2,0:T(8,128)(2,1)}, bf16[1280,1280]{1,0:T(8,128)(2,1)}), (bf16[3,1280,320]{1,2,0:T(8,128)(2,1)}, ...) | async-done | bytes 13107216 | tf_op jit(solution)/shard_map/psum | solution.py:179
  1041.0 5.8 convert_multiply_fusion
  1046.8 13.9 %copy.54 = f32[2,1280,1280]{2,1,0:T(8,128)} copy(f32[2,1280,1280]{1,2,0:T(8,128)} %convert_multiply_fusion) | data formatting | bytes 26214400
  (171 shorter events, 140.0 us)
Async XLA Ops:
  7.2 4.1 copy-start.31
  7.2 49.1 %all-gather.5.cloned.1.call-start = ((), (), s32[]{:S(2)}) async-start(), calls=%async_computation.4 | async-start | bytes 6553600 | tf_op jit(solution)/shard_map/all_gather | solution.py:85
  8.1 4.9 copy-start.35
  11.3 190.5 %copy-start.4 = (f32[512,1280]{1,0:T(8,128)}, f32[512,1280]{1,0:T(8,128)S(1)}, u32[]{:S(2)}) copy-start(f32[512,1280]{1,0:T(8,128)S(1)} %get-tuple-element.77) | copy-start | bytes 7864324
  13.0 188.8 %reduce-scatter.5.cloned.1.call-start = ((), (), s32[]{:S(2)}) async-start(), calls=%async_computation.5 | async-start | bytes 6553600 | tf_op jit(solution)/shard_map/reduce_scatter | solution.py:102
  127.9 3.3 copy-start.8
  127.9 3.3 copy-start.14
  131.2 4.3 copy-start.2
  150.2 54.8 %copy-start.30 = (f32[1280]{0:T(1024)S(1)}, f32[1280]{0:T(1024)}, u32[]{:S(2)}) copy-start(f32[1280]{0:T(1024)} %param.16) | copy-start | bytes 15364
  150.2 96.8 %all-gather.7.cloned.1.call-start = ((), (), s32[]{:S(2)}) async-start(), calls=%async_computation.6 | async-start | bytes 6553600 | tf_op jit(solution)/shard_map/all_gather | solution.py:106
  203.6 3.7 copy-start.18
  206.4 83.1 %all-gather.9.cloned.1.call-start = ((), (), s32[]{:S(2)}) async-start(), calls=%async_computation.8 | async-start | bytes 6553600 | tf_op jit(solution)/shard_map/all_gather | solution.py:120
  208.5 176.0 %reduce-scatter.9.cloned.1.call-start = ((), (), s32[]{:S(2)}) async-start(), calls=%async_computation.9 | async-start | bytes 6553600 | tf_op jit(solution)/shard_map/reduce_scatter | solution.py:134
  333.0 105.4 %reduce-scatter.7.cloned.1.call-start = ((), (), s32[]{:S(2)}) async-start(), calls=%async_computation.7 | async-start | bytes 6553600 | tf_op jit(solution)/shard_map/reduce_scatter | solution.py:116
  345.4 39.2 %copy-start.7 = (f32[512,1280]{1,0:T(8,128)S(1)}, f32[512,1280]{1,0:T(8,128)}, u32[]{:S(2)}) copy-start(f32[512,1280]{1,0:T(8,128)} %copy-done.6) | copy-start | bytes 7864324
  345.4 139.9 %all-gather.11.cloned.1.call-start = ((), (), s32[]{:S(2)}) async-start(), calls=%async_computation.10 | async-start | bytes 6553600 | tf_op jit(solution)/shard_map/all_gather | solution.py:139
  444.7 167.3 %reduce-scatter.11.cloned.1.call-start = ((), (), s32[]{:S(2)}) async-start(), calls=%async_computation.11 | async-start | bytes 6553600 | tf_op jit(solution)/shard_map/reduce_scatter | solution.py:169
  497.8 4.5 copy-start.3
  497.8 4.5 copy-start.21
  560.4 470.0 %all-reduce.5.cloned.1.call-start = ((), (), s32[]{:S(2)}) async-start(), calls=%async_computation.12 | async-start | bytes 26214400 | tf_op jit(solution)/shard_map/psum | solution.py:179
  560.4 32.6 %slice-start.4 = ((s8[5242880]{0:T(1024)(128)(4,1)}), s8[4194304]{0:T(1024)(128)(4,1)S(1)}, s32[]{:S(2)}) async-start(s8[5242880]{0:T(1024)(128)(4,1)} %bitcast.110), calls=%async_computation.17 | async-start | bytes 8388608
  560.5 35.5 %slice-start.2 = ((s8[5242880]{0:T(1024)(128)(4,1)}), s8[4194304]{0:T(1024)(128)(4,1)S(1)}, s32[]{:S(2)}) async-start(s8[5242880]{0:T(1024)(128)(4,1)} %bitcast.108), calls=%async_computation.15 | async-start | bytes 8388608
  572.8 20.3 %copy-start.27 = (bf16[2048,320]{1,0:T(8,128)(2,1)S(1)}, bf16[2048,320]{1,0:T(8,128)(2,1)}, u32[]{:S(2)}) copy-start(bf16[2048,320]{1,0:T(8,128)(2,1)} %convert_element_type.131) | copy-start | bytes 3932164
  572.8 20.3 %slice-start.5 = ((s8[5242880]{0:T(1024)(128)(4,1)}), s8[1048576]{0:T(1024)(128)(4,1)S(1)}, s32[]{:S(2)}) async-start(s8[5242880]{0:T(1024)(128)(4,1)} %bitcast.110), calls=%async_computation.18 | async-start | bytes 2097152
  572.8 23.1 %slice-start.3 = ((s8[5242880]{0:T(1024)(128)(4,1)}), s8[1048576]{0:T(1024)(128)(4,1)S(1)}, s32[]{:S(2)}) async-start(s8[5242880]{0:T(1024)(128)(4,1)} %bitcast.108), calls=%async_computation.16 | async-start | bytes 2097152
  602.5 9.5 copy-start.5
  602.5 9.5 copy-start.32
  602.5 9.5 copy-start.34
  1032.9 3.3 copy-start.25
  1033.0 7.0 slice-start
  1036.2 4.7 slice-start.1
  1046.8 13.9 %copy-start.1 = (f32[3,1280]{1,0:T(4,128)S(1)}, f32[3,1280]{1,0:T(4,128)}, u32[]{:S(2)}) copy-start(f32[3,1280]{1,0:T(4,128)} %param.14) | copy-start | bytes 46084
  (21 other events, 45.5 us)
Sparse Core Ops, SparseCore 0:
  13.1 43.1 all-gather.4
  150.4 51.3 reduce-scatter.4
  206.5 40.4 all-gather.6
  249.1 40.4 all-gather.8
  333.1 51.3 reduce-scatter.8
  386.9 51.3 reduce-scatter.6
  444.8 40.4 all-gather.10
  560.5 51.3 reduce-scatter.10
  617.3 412.9 all-reduce.4
